TPU v7x, 32 devices: a whole 2x2x4 slice. The times are simulated.
32 devices in a mesh: samp: 8 (over y, x, core), cls: 4 (over z).
Axes of the slice: x: 2, y: 2, z: 4, core: 2. Of those that a mesh axis runs over, the one named last changes fastest.
Arguments:
- samples: bfloat16 [1024, 32768], P('samp'), may hold values from -0.046875 to 0.046875
- labels: int32 [1024], P('samp'), may hold values from 0 to 511
- weight: bfloat16 [32768, 512], P('samp', 'cls'), may hold values from -6 to 6
- dual: float32 [1024, 512], P('samp', 'cls'), may hold values from 0 to 1
- block_inverse: float32 [64, 16, 16], P('samp'), may hold values from -0.4 to 1.2, as said below
Outputs:
- new_weight: float32 [32768, 512], P('samp', 'cls')
- new_dual: float32 [1024, 512], P('samp', 'cls')
- class_gap: float32 [512], P('cls')
- top_margin: float32 [1024], P('samp')
Inputs may be any that keep to these rules, and one draw needn't show every extreme that they name: `block_inverse`: each [16, 16] matrix has a positive diagonal.
All inputs are finite; a program needn't handle non-finite values.
Results may differ from a plain program's by a relative error of at most 0.00045.
Values may be sent and summed in bfloat16 or wider, within the bound.
A program may use at most 128 MiB of HBM per device.

v0:
```python
import jax
import jax.numpy as jnp
from jax import lax
from jax.sharding import PartitionSpec as P

BLOCK = 16
PASSES = 2


coupling = 0.5


def dual_passes(gram, start, sign, dual, inverse):
    rows = start.shape[0]
    blocks = rows // BLOCK

    def visit(turn, carry):
        alpha, change = carry
        index = (turn % blocks).astype(jnp.int32)
        low = index * BLOCK
        gram_rows = lax.dynamic_slice_in_dim(gram, low, BLOCK, 0)
        start_rows = lax.dynamic_slice_in_dim(start, low, BLOCK, 0)
        sign_rows = lax.dynamic_slice_in_dim(sign, low, BLOCK, 0)
        dual_rows = lax.dynamic_slice_in_dim(dual, low, BLOCK, 0)
        alpha_rows = lax.dynamic_slice_in_dim(alpha, low, BLOCK, 0)
        matrix = lax.dynamic_index_in_dim(inverse, index, 0, keepdims=False)
        margin = start_rows + coupling * jnp.dot(gram_rows, change, precision=lax.Precision.HIGHEST)
        ascent = jnp.dot(matrix, 1.0 - sign_rows * margin, precision=lax.Precision.HIGHEST)
        alpha_rows = jnp.clip(alpha_rows + ascent, 0.0, 1.0)
        change_rows = sign_rows * (alpha_rows - dual_rows)
        alpha = lax.dynamic_update_slice_in_dim(alpha, alpha_rows, low, 0)
        change = lax.dynamic_update_slice_in_dim(change, change_rows, low, 0)
        return (alpha, change)

    alpha, change = lax.fori_loop(0, PASSES * blocks, visit, (dual, jnp.zeros_like(dual)))
    margin = start + coupling * jnp.dot(gram, change, precision=lax.Precision.HIGHEST)
    return (alpha, margin, change)


def body(samples, labels, weight, dual, block_inverse):
    rows, features = samples.shape
    width = weight.shape[1]
    class_ids = lax.axis_index("cls") * width + jnp.arange(width, dtype=jnp.int32)
    sign = jnp.where(labels[:, None] == class_ids[None, :], 1.0, -1.0).astype(jnp.float32)
    columns = samples
    start = jnp.dot(
        columns,
        lax.all_gather(weight, "samp", axis=0, tiled=True),
        preferred_element_type=jnp.float32,
    )
    gram = lax.dot_general(
        samples, samples, (((1,), (1,)), ((), ())), preferred_element_type=jnp.float32
    )
    scaled = sign * start
    terms = jnp.maximum(0.0, 1.0 - scaled) + dual * (scaled - 1.0)
    class_gap = lax.psum(jnp.sum(terms, axis=0), "samp") / (rows * lax.axis_size("samp"))
    alpha, margin, change = dual_passes(gram, start, sign, dual, block_inverse)
    top_margin = lax.pmax(jnp.max(margin, axis=1), "cls")
    steps = change.astype(jnp.bfloat16)
    columns = samples
    delta = lax.psum_scatter(
        lax.dot_general(
            columns, steps, (((0,), (0,)), ((), ())), preferred_element_type=jnp.float32
        ),
        "samp",
        scatter_dimension=0,
        tiled=True,
    )
    new_weight = weight.astype(jnp.float32) + coupling * delta
    return (new_weight, alpha, class_gap, top_margin)


def solution(mesh):
    placed = (P("samp", None), P("samp"), P("samp", "cls"), P("samp", "cls"), P("samp", None, None))
    return jax.shard_map(
        body,
        mesh=mesh,
        in_specs=placed,
        out_specs=(P("samp", "cls"), P("samp", "cls"), P("cls"), P("samp")),
        check_vma=False,
    )
```

profile of v0, /device:TPU:0, one launch (start us, length us, event | category | flops | bytes accessed | tf_op | source)
XLA Modules:
  0.0 230.1 jit_solution(18239137060779799325)
XLA Ops:
  7.2 0.0 all-gather.2.cloned.1.call-start
  7.2 0.7 all-gather.2.cloned.1.call-update
  7.9 0.0 reduce-scatter.2.cloned.1.call-start
  7.9 0.8 copy.16
  8.8 0.0 copy-start.1
  8.8 0.0 copy-start.3
  8.8 8.1 %fusion.12 = f32[128,128]{1,0:T(8,128)S(1)} fusion(bf16[128,32768]{1,0:T(8,128)(2,1)} %param.7), kind=kOutput, calls=%fused_computation.23 | convolution fusion | flops 1073741824 | bytes 8454144 | tf_op jit(solution)/shard_map/dot_general | solution.py:51
  16.9 50.0 %all-gather.2.cloned.1.call-done = bf16[32768,128]{1,0:T(8,128)(2,1)} async-done(((bf16[4096,128]{1,0:T(8,128)(2,1)}), bf16[32768,128]{1,0:T(8,128)(2,1)}) %all-gather.2.cloned.1.call-update) | async-done | bytes 8388624 | tf_op jit(solution)/shard_map/all_gather | solution.py:48
  66.9 0.0 copy-done.1
  66.9 0.0 copy-done.3
  66.9 8.1 %add_reduce_fusion = (f32[128]{0:T(128)S(1)}, f32[128,128]{1,0:T(8,128)S(1)}, f32[128,128]{1,0:T(8,128)S(1)}) fusion(f32[128,128]{1,0:T(8,128)S(1)} %copy-done.1, s32[128]{0:T(128)S(1)} %iota_add_fusion, s32[128]{0:T(128)S(1)} %copy-done.3, bf16[128,32768]{1,0:T(8,128)(2,1)} %param.7, bf16[32768,128]{1,0:T(8,128)(2,1)} %all-gather.2.cloned.1.call-done), kind=kOutput, calls=%fused_computation.18 | convolution fusion | flops 1073889152 | bytes 16975360 | tf_op jit(solution)/shard_map/dot_general | solution.py:46
  75.0 16.8 %while.17 = (s32[]{:T(128)}, f32[128,128]{1,0:T(8,128)S(1)}, f32[128,128]{1,0:T(8,128)S(1)}, f32[8,16,16]{2,1,0:T(8,128)}, f32[128,128]{1,0:T(8,128)S(1)}, /*ind...) while((s32[]{:T(128)}, f32[128,128]{1,0:T(8,128)S(1)}, ...), condition=%wide.region_1.2_spmd, body=%wide.region_0.1_spmd.sunk | while | flops 3555343 | bytes 173339 | solution.py:35
  75.1 0.2 fusion.32
  75.2 0.8 fusion.33
  76.1 0.2 fusion.32
  76.3 0.8 fusion.33
  77.2 0.2 fusion.32
  77.3 0.8 fusion.33
  78.2 0.2 fusion.32
  78.4 0.8 fusion.33
  79.2 0.2 fusion.32
  79.4 0.8 fusion.33
  80.3 0.2 fusion.32
  80.5 0.8 fusion.33
  81.3 0.2 fusion.32
  81.5 0.8 fusion.33
  82.4 0.2 fusion.32
  82.6 0.8 fusion.33
  83.4 0.2 fusion.32
  83.6 0.8 fusion.33
  84.5 0.2 fusion.32
  84.7 0.8 fusion.33
  85.5 0.2 fusion.32
  85.7 0.8 fusion.33
  86.6 0.2 fusion.32
  86.8 0.8 fusion.33
  87.6 0.2 fusion.32
  87.8 0.8 fusion.33
  88.7 0.2 fusion.32
  88.9 0.8 fusion.33
  89.7 0.2 fusion.32
  89.9 0.8 fusion.33
  90.8 0.2 fusion.32
  91.0 0.8 fusion.33
  91.8 0.0 copy-start.2
  91.8 11.5 %convolution_bitcast_fusion = f32[32768,128]{0,1:T(8,128)} fusion(bf16[128,32768]{1,0:T(8,128)(2,1)} %param.7, f32[128,128]{1,0:T(8,128)S(1)} %get-tuple-element.204), kind=kOutput, calls=%fused_computation.13 | convolution fusion | flops 1073758208 | bytes 25231360 | tf_op jit(solution)/shard_map/dot_general | solution.py:62
  103.3 0.0 copy-done.2
  103.3 0.0 copy-start
  103.3 0.0 reduce-scatter.2.cloned.1.call-update
  103.4 1.2 copy-done
  104.6 0.5 copy.9
  105.1 13.1 %psum.7 = f32[128]{0:T(128)S(1)} all-reduce(f32[128]{0:T(128)S(1)} %get-tuple-element.228), channel_id=1, replica_groups=mesh['samp'=8,'cls'=4] {'samp'}, use_global_device_ids=true, to_apply=%region_4.5 | all-reduce | flops 128 | bytes 1024 | tf_op jit(solution)/shard_map/psum | solution.py:56
  118.2 0.3 fusion.10
  118.5 12.2 %pmax.7 = f32[128]{0:T(128)} all-reduce(f32[128]{0:T(128)S(1)} %fusion.10), channel_id=1, replica_groups=mesh['samp'=8,'cls'=4] {'cls'}, use_global_device_ids=true, to_apply=%region_6.7 | all-reduce | flops 128 | bytes 1024 | tf_op jit(solution)/shard_map/pmax | solution.py:58
  130.7 0.5 broadcast_multiply_fusion
  131.2 88.4 %reduce-scatter.2.cloned.1.call-done = f32[4096,128]{0,1:T(8,128)} async-done(((f32[32768,128]{0,1:T(8,128)}), f32[4096,128]{0,1:T(8,128)}) %reduce-scatter.2.cloned.1.call-update) | async-done | bytes 2097168 | tf_op jit(solution)/shard_map/reduce_scatter | solution.py:61
  219.6 1.9 multiply_add_fusion
  221.5 1.8 copy.11
  (18 shorter events, 0.1 us)
Async XLA Ops:
  7.2 59.7 %all-gather.2.cloned.1.call-start = ((), (), s32[]{:S(2)}) async-start(), calls=%async_computation.1 | async-start | bytes 9437184 | tf_op jit(solution)/shard_map/all_gather | solution.py:48
  7.9 211.7 %reduce-scatter.2.cloned.1.call-start = ((), (), s32[]{:S(2)}) async-start(), calls=%async_computation.2 | async-start | bytes 18874368 | tf_op jit(solution)/shard_map/reduce_scatter | solution.py:61
  8.8 58.1 %copy-start.1 = (f32[128,128]{1,0:T(8,128)S(1)}, f32[128,128]{1,0:T(8,128)}, u32[]{:S(2)}) copy-start(f32[128,128]{1,0:T(8,128)} %param.10) | copy-start | bytes 196612
  8.8 58.1 %copy-start.3 = (s32[128]{0:T(128)S(1)}, s32[128]{0:T(128)}, u32[]{:S(2)}) copy-start(s32[128]{0:T(128)} %param.8) | copy-start | bytes 1540
  91.8 11.5 %copy-start.2 = (f32[128,128]{1,0:T(8,128)}, f32[128,128]{1,0:T(8,128)S(1)}, u32[]{:S(2)}) copy-start(f32[128,128]{1,0:T(8,128)S(1)} %get-tuple-element.207) | copy-start | bytes 196612
  103.3 1.2 copy-start
Sparse Core Ops, SparseCore 0:
  9.9 56.9 all-gather.1
  103.5 116.0 reduce-scatter.1
where the time goes:
time: 231 us; the launch traced here: 230 us
  waiting for transfers between devices  139 us (60%)
  matrix products  44.2 us (19%)
  blocking collectives  25.3 us (11%)
  between operations  14.1 us (6%)
  local copies, waits for them, and re-layouts  4.4 us (2%)
  other arithmetic  2.5 us (1%)
    reduce_scatter x1, waiting for transfers between devices, body(): lax.psum_scatter(lax.dot_general(columns, steps, (((0,), (0,)), ((), ()))...  88.4 us
    all_gather x1, waiting for transfers between devices, body(): lax.all_gather(weight, 'samp', axis=0, tiled=True)  50 us
    dot_general x16, matrix products, visit(): jnp.dot(matrix, 1.0 - sign_rows * margin, precision=lax.Precision.HIGHEST)  13.4 us
    psum x1, blocking collectives, body(): lax.psum(jnp.sum(terms, axis=0), 'samp') / (rows * lax.axis_size('samp'))  13.1 us
    pmax x1, blocking collectives, body(): top_margin = lax.pmax(jnp.max(margin, axis=1), 'cls')  12.2 us
    dot_general x1, matrix products, body(): lax.dot_general(columns, steps, (((0,), (0,)), ((), ())), preferred_eleme...  11.5 us
    dot_general x1, matrix products, body(): lax.dot_general(samples, samples, (((1,), (1,)), ((), ())), preferred_ele...  8.12 us
    dot_general x1, matrix products, body(): jnp.dot(columns, lax.all_gather(weight, 'samp', axis=0, tiled=True), pref...  8.12 us
  transfers between devices with their start and end apart: 2, of which 2 were waited for; matrix products, arithmetic and copies ran while one was open for 4% of the time, Pallas kernels for 0%

commit v1 on v0

v1 whole, which is shorter than its diff:
```python
import functools

import jax
import jax.numpy as jnp
from jax import lax
from jax.experimental import pallas as pl
from jax.experimental.pallas import tpu as pltpu
from jax.sharding import PartitionSpec as P

PASSES = 2
coupling = 0.5
MESH = pl.DeviceIdType.MESH
SUBS = 2
F32 = jnp.float32


def flip(index, mask, n):
    out = 0
    bit = 1
    while bit < n:
        digit = (index // bit) % 2
        if mask & bit:
            digit = 1 - digit
        out = out + digit * bit
        bit *= 2
    return out


def shares(d, F, split):
    hops = bin(d >> 1).count("1")
    if not split or hops == 0:
        return 0
    if hops == 1:
        return max(F * 5 // 16 // 128 * 128, 128)
    return F // 2 // 128 * 128


def kernel(n, ncls, BLOCK, samples, labels_col, weight, dual, inverse,
           new_weight, new_dual, class_gap, top_margin,
           a_all, x_buf, w_buf, gb, ib, gram, margin, sign, dual_v, alpha, change, inv_v, lab_v,
           p_buf, r_buf, gap_out, gap_in, top_out, top_in, s_out, s_all, o_buf,
           send_split, recv_split, send_fwd, recv_fwd, send_direct, recv_direct,
           x_sem, in_sem, send_p, recv_p, send_g, recv_g, send_t, recv_t, send_s, recv_s, out_sem):
    s = lax.axis_index("samp")
    c = lax.axis_index("cls")
    rows, N = samples.shape
    F = N // n
    width = weight.shape[1]
    par = c % 2
    pair = c + 1 - 2 * par
    split = ncls % 2 == 0
    peer = {d: flip(s, d, n) for d in range(1, n)}
    step_rows = rows // SUBS

    barrier = pltpu.get_barrier_semaphore()
    for d in range(1, n):
        pl.semaphore_signal(barrier, inc=1, device_id=(peer[d], c), device_id_type=MESH)
    for j in range(1, ncls):
        pl.semaphore_signal(barrier, inc=1, device_id=(s, (c + j) % ncls), device_id_type=MESH)
    pl.semaphore_wait(barrier, n - 1 + ncls - 1)

    def remote(src, dst, ssem, rsem, dev):
        return pltpu.make_async_remote_copy(src_ref=src, dst_ref=dst, send_sem=ssem, recv_sem=rsem,
                                            device_id=dev, device_id_type=MESH)

    def cols(start, size):
        return pl.ds(pl.multiple_of(start, 128), size)

    one_hop = [d for d in range(1, n) if bin(d >> 1).count("1") == 1]
    far = [d for d in range(1, n) if bin(d >> 1).count("1") > 1]
    near = [d for d in range(1, n) if d >> 1 == 0]
    one_hop = [d for d in one_hop if d % 2 == 0] + [d for d in one_hop if d % 2]
    order = [(d, k) for d in one_hop for k in range(SUBS)]
    order = sorted(order, key=lambda e: (e[1], one_hop.index(e[0])))
    order = order + [(d, k) for d in far for k in range(SUBS)]
    order = [e for e in order if shares(e[0], F, split)]
    finals = []

    split_copy, fwd_copy, direct_copy = {}, {}, {}
    for d, k in order:
        h = shares(d, F, split)
        rs = pl.ds(k * step_rows, step_rows)
        copy = remote(samples.at[rs, cols(peer[d] * F + par * h, h)],
                      a_all.at[s, rs, cols(par * h, h)],
                      send_split.at[d, k], recv_split.at[d, k], (peer[d], c))
        copy.start()
        split_copy[d, k] = copy
    for d in near + one_hop + far:
        h = shares(d, F, split)
        if 2 * h < F:
            copy = remote(samples.at[:, cols(peer[d] * F + 2 * h, F - 2 * h)],
                          a_all.at[s, :, 2 * h:F],
                          send_direct.at[d], recv_direct.at[d], (peer[d], c))
            copy.start()
            direct_copy[d] = copy

    loads = []
    for i, (src, dst) in enumerate([(samples.at[:, cols(s * F, F)], a_all.at[s]), (weight, w_buf),
                                    (dual, dual_v), (inverse, inv_v), (labels_col, lab_v)]):
        load = pltpu.make_async_copy(src, dst, in_sem.at[i])
        load.start()
        loads.append(load)
    x_loads = []
    for i in range(n):
        load = pltpu.make_async_copy(samples.at[:, i * F:(i + 1) * F], x_buf.at[i], x_sem.at[i])
        load.start()
        x_loads.append(load)

    def gram_piece(i):
        x_loads[i].wait()
        x = x_buf[i]
        part = lax.dot_general(x, x, (((1,), (1,)), ((), ())), preferred_element_type=F32)
        gram[...] = part if i == 0 else gram[...] + part

    def broadcast_piece(i):
        g = coupling * gram[...]
        for k in range(i * BLOCK, (i + 1) * BLOCK):
            gb[k] = jnp.broadcast_to(g[:, k:k + 1], (rows, width))

    def inverse_piece():
        for k in range(BLOCK):
            ib[k] = jnp.broadcast_to(inv_v[:, k:k + 1], (rows, width))
        ids = c * width + lax.broadcasted_iota(jnp.int32, (rows, width), 1)
        sign[...] = jnp.where(lab_v[...] == ids, 1.0, -1.0).astype(F32)
        alpha[...] = dual_v[...]
        change[...] = jnp.zeros((rows, width), F32)

    def own_piece():
        p_buf[0] = jnp.dot(a_all[s], w_buf[...], preferred_element_type=F32)

    work = [functools.partial(gram_piece, i) for i in range(n)]
    work += [own_piece, inverse_piece]
    work += [functools.partial(broadcast_piece, i) for i in range(rows // BLOCK)]
    per = -(-len(work) // max(len(order), 1))

    partial_copy = {}

    def partial_of(d):
        if d in direct_copy:
            direct_copy[d].wait_recv()
        if shares(d, F, split):
            for k in range(SUBS):
                fwd_copy[d, k].wait_recv()
        p_buf[d] = jnp.dot(a_all[peer[d]], w_buf[...], preferred_element_type=F32)
        copy = remote(p_buf.at[d], r_buf.at[d], send_p.at[d], recv_p.at[d], (peer[d], c))
        copy.start()
        partial_copy[d] = copy

    for load in loads:
        load.wait()
    for d, k in order:
        h = shares(d, F, split)
        rs = pl.ds(k * step_rows, step_rows)
        split_copy[d, k].wait_recv()
        src = a_all.at[peer[d], rs, cols(par * h, h)]
        copy = remote(src, src, send_fwd.at[d, k], recv_fwd.at[d, k], (s, pair))
        copy.start()
        fwd_copy[d, k] = copy
        for _ in range(per):
            if work:
                work.pop(0)()
    while work:
        work.pop(0)()
    for d in near + one_hop + far:
        partial_of(d)

    start = p_buf[0]
    for d in range(1, n):
        partial_copy[d].wait_recv()
        start = start + r_buf[d]
    margin[...] = start
    scaled = sign[...] * start
    terms = jnp.maximum(0.0, 1.0 - scaled) + dual_v[...] * (scaled - 1.0)
    gap = jnp.sum(terms, axis=0, keepdims=True)
    gap_out[...] = jnp.broadcast_to(gap, gap_out.shape)
    gap_copy = []
    for d in range(1, n):
        copy = remote(gap_out, gap_in.at[d], send_g.at[d], recv_g.at[d], (peer[d], c))
        copy.start()
        gap_copy.append(copy)

    blocks = rows // BLOCK

    def visit(turn, carry):
        low = pl.multiple_of((turn % blocks) * BLOCK, BLOCK)
        here = pl.ds(low, BLOCK)
        sign_b = sign[here, :]
        residual = 1.0 - sign_b * margin[here, :]
        ascent = jnp.zeros((BLOCK, width), F32)
        for k in range(BLOCK):
            ascent = ascent + ib[k, here, :] * residual[k:k + 1, :]
        alpha_b = jnp.clip(alpha[here, :] + ascent, 0.0, 1.0)
        change_b = sign_b * (alpha_b - dual_v[here, :])
        moved = change_b - change[here, :]
        alpha[here, :] = alpha_b
        change[here, :] = change_b
        total = margin[...]
        for k in range(BLOCK):
            total = total + gb[low + k] * moved[k:k + 1, :]
        margin[...] = total
        return carry

    lax.fori_loop(0, PASSES * blocks, visit, 0)

    s_out[...] = change[...].astype(jnp.bfloat16)
    step_copy = []
    for d in far + one_hop + near:
        copy = remote(s_out, s_all.at[s], send_s.at[d], recv_s.at[d], (peer[d], c))
        copy.start()
        step_copy.append(copy)
    s_all[s] = s_out[...]
    top = jnp.max(margin[...].T, axis=0, keepdims=True)
    top_out[...] = jnp.broadcast_to(top, top_out.shape)
    top_copy = []
    for j in range(1, ncls):
        copy = remote(top_out, top_in.at[j], send_t.at[j], recv_t.at[j], (s, (c + j) % ncls))
        copy.start()
        top_copy.append(copy)
    dual_store = pltpu.make_async_copy(alpha, new_dual, out_sem.at[0])
    dual_store.start()
    for copy in step_copy:
        copy.wait_recv()
    steps = s_all[...].reshape(n * rows, width)
    chunks = o_buf.shape[0]
    tile = F // chunks
    stores = []
    for i in range(chunks):
        a = a_all[:, :, i * tile:(i + 1) * tile].reshape(n * rows, tile)
        delta = lax.dot_general(a, steps, (((0,), (0,)), ((), ())), preferred_element_type=F32)
        o_buf[i] = w_buf[i * tile:(i + 1) * tile, :].astype(F32) + coupling * delta
        store = pltpu.make_async_copy(o_buf.at[i], new_weight.at[i * tile:(i + 1) * tile, :], out_sem.at[1 + i])
        store.start()
        stores.append(store)

    gap_sum = gap
    for d, copy in zip(range(1, n), gap_copy):
        copy.wait_recv()
        gap_sum = gap_sum + gap_in[d, 0:1, :]
    class_gap[...] = gap_sum / (rows * n)
    best = top
    for j, copy in zip(range(1, ncls), top_copy):
        copy.wait_recv()
        best = jnp.maximum(best, top_in[j, 0:1, :])
    top_margin[...] = best

    for copy in (list(split_copy.values()) + list(fwd_copy.values()) + list(direct_copy.values())
                 + list(partial_copy.values()) + gap_copy + step_copy + top_copy):
        copy.wait_send()
    dual_store.wait()
    for store in stores:
        store.wait()


def fused(n, ncls, samples, labels, weight, dual, block_inverse):
    rows, N = samples.shape
    F, width = weight.shape
    block = block_inverse.shape[1]
    inverse = block_inverse.reshape(rows, block)
    any_spec = pl.BlockSpec(memory_space=pl.ANY)
    vmem = pl.BlockSpec(memory_space=pltpu.VMEM)
    chunks = max(F // 512, 1)
    square = pltpu.VMEM((rows, width), F32)
    dma = pltpu.SemaphoreType.DMA
    outs = pl.pallas_call(
        functools.partial(kernel, n, ncls, block),
        out_shape=(jax.ShapeDtypeStruct((F, width), F32), jax.ShapeDtypeStruct((rows, width), F32),
                   jax.ShapeDtypeStruct((1, width), F32), jax.ShapeDtypeStruct((1, rows), F32)),
        in_specs=[any_spec] * 5,
        out_specs=(any_spec, any_spec, vmem, vmem),
        scratch_shapes=[
            pltpu.VMEM((n, rows, F), jnp.bfloat16), pltpu.VMEM((n, rows, F), jnp.bfloat16),
            pltpu.VMEM((F, width), jnp.bfloat16),
            pltpu.VMEM((rows, rows, width), F32), pltpu.VMEM((block, rows, width), F32),
            pltpu.VMEM((rows, rows), F32), square, square, square, square, square,
            pltpu.VMEM((rows, block), F32), pltpu.VMEM((rows, 1), jnp.int32),
            pltpu.VMEM((n, rows, width), F32), pltpu.VMEM((n, rows, width), F32),
            pltpu.VMEM((8, width), F32), pltpu.VMEM((n, 8, width), F32),
            pltpu.VMEM((8, rows), F32), pltpu.VMEM((ncls, 8, rows), F32),
            pltpu.VMEM((rows, width), jnp.bfloat16), pltpu.VMEM((n, rows, width), jnp.bfloat16),
            pltpu.VMEM((chunks, F // chunks, width), F32),
            dma((n, SUBS)), dma((n, SUBS)), dma((n, SUBS)), dma((n, SUBS)), dma((n,)), dma((n,)),
            dma((n,)), dma((5,)), dma((n,)), dma((n,)), dma((n,)), dma((n,)), dma((ncls,)), dma((ncls,)),
            dma((n,)), dma((n,)), dma((1 + chunks,)),
        ],
        compiler_params=pltpu.CompilerParams(collective_id=0, has_side_effects=True,
                                             vmem_limit_bytes=60 * 2 ** 20),
    )(samples, labels[:, None], weight, dual, inverse)
    new_weight, new_dual, gap, top = outs
    return new_weight, new_dual, gap.reshape(-1), top.reshape(-1)


def solution(mesh):
    n, ncls = mesh.shape["samp"], mesh.shape["cls"]
    placed = (P("samp", None), P("samp"), P("samp", "cls"), P("samp", "cls"), P("samp", None, None))
    return jax.shard_map(
        functools.partial(fused, n, ncls),
        mesh=mesh,
        in_specs=placed,
        out_specs=(P("samp", "cls"), P("samp", "cls"), P("cls"), P("samp")),
        check_vma=False,
    )
```

time: 231 us -> 86 us (0.37)
  waiting for transfers between devices: 139 us -> 0 us
  Pallas kernels: 0 us -> 79.1 us
  matrix products: 44.2 us -> 0 us
  blocking collectives: 25.3 us -> 0 us
  between operations: 14.1 us -> 0.67 us
  other arithmetic: 2.5 us -> 0 us
    reduce_scatter x1 -> x0, waiting for transfers between devices: 88.4 us -> none  [body(): lax.psum_scatter(lax.dot_general(columns, steps, (((0,), (0,)), ((), ()))...]
    pallas_call x0 -> x1, Pallas kernels: none -> 79.1 us  [fused(): pl.pallas_call(functools.partial(kernel, n, ncls, block), out_shape=(jax....]
    all_gather x1 -> x0, waiting for transfers between devices: 50 us -> none  [body(): lax.all_gather(weight, 'samp', axis=0, tiled=True)]
    dot_general x36 -> x0, matrix products: 44.2 us -> none  [the longest x16 13.4 us: visit(): jnp.dot(matrix, 1.0 - sign_rows * margin, precision=lax.Precision.HIGHEST)]
    psum x1 -> x0, blocking collectives: 13.1 us -> none  [body(): lax.psum(jnp.sum(terms, axis=0), 'samp') / (rows * lax.axis_size('samp'))]
    pmax x1 -> x0, blocking collectives: 12.2 us -> none  [body(): top_margin = lax.pmax(jnp.max(margin, axis=1), 'cls')]
    unnamed x11 -> x10, local copies, waits for them, and re-layouts: 4.39 us -> 4.72 us
  transfers between devices with their start and end apart: 2 -> 0, of which waited for: 2 -> 0; matrix products, arithmetic and copies ran while one was open for 4% -> 0% of each run, Pallas kernels for 0% -> 0%
where the time goes in v1:
time: 86 us; the launch traced here: 85.8 us
  Pallas kernels  79.1 us (92%)
  local copies, waits for them, and re-layouts  6.11 us (7%)
    pallas_call x1, Pallas kernels, fused(): pl.pallas_call(functools.partial(kernel, n, ncls, block), out_shape=(jax....  79.1 us
    unnamed x10, local copies, waits for them, and re-layouts  4.72 us

profile of v1, /device:TPU:0, one launch (start us, length us, event | category | flops | bytes accessed | tf_op | source)
XLA Modules:
  0.0 85.8 jit_solution(3986891389218068791)
XLA Ops:
  0.6 1.4 %copy.9.labels_col = s32[128,1]{1,0:T(8,128)} copy(s32[128,1]{0,1:T(1,128)} %bitcast.5) | data formatting | bytes 1024 | tf_op jit(solution)/shard_map/broadcast_in_dim | solution.py:287
  2.0 79.1 %shard_map.84 = (f32[4096,128]{1,0:T(8,128)}, f32[128,128]{1,0:T(8,128)}, f32[1,128]{1,0:T(1,128)}, f32[1,128]{1,0:T(1,128)}) custom-call(bf16[128,32768]{1,0:T(8,128)(2,1)} %samples.1, s32[128,1]{1,0:T(8,128)} %copy.9.labels_col, bf16[4096,128]{1,0:T(8,128)(2,1)} %weight.1, f32[128,128]{1,0:T(8,128)} %dual.1, f32[128,16]{1,0:T(8,128)} %bitcast.4), custom_call_target="tpu_custom_call" | custom-call | tf_op jit(solution)/shard_map/pallas_call | solution.py:264
  81.1 0.0 copy-start
  81.1 0.0 copy-start.2
  81.1 0.0 copy-start.1
  81.1 3.1 %copy.14 = f32[4096,128]{1,0:T(8,128)} copy(f32[4096,128]{1,0:T(8,128)} %get-tuple-element.16) | data formatting | bytes 4194304
  84.2 0.0 copy-done
  84.2 0.6 copy.15
  84.8 0.0 copy-done.2
  84.8 0.5 copy.16
  85.3 0.0 copy-done.1
  85.3 0.5 copy.17
Async XLA Ops:
  81.1 3.1 %copy-start = (f32[128,128]{1,0:T(8,128)S(1)}, f32[128,128]{1,0:T(8,128)}, u32[]{:S(2)}) copy-start(f32[128,128]{1,0:T(8,128)} %get-tuple-element.17) | copy-start | bytes 196612
  81.1 3.7 %copy-start.2 = (f32[1,128]{1,0:T(1,128)S(1)}, f32[1,128]{1,0:T(1,128)}, u32[]{:S(2)}) copy-start(f32[1,128]{1,0:T(1,128)} %get-tuple-element.10) | copy-start | bytes 1540
  81.1 4.2 %copy-start.1 = (f32[1,128]{1,0:T(1,128)S(1)}, f32[1,128]{1,0:T(1,128)}, u32[]{:S(2)}) copy-start(f32[1,128]{1,0:T(1,128)} %get-tuple-element.11) | copy-start | bytes 1540

commit v2 on v1

--- a/solution.py
+++ b/solution.py
@@ -11,6 +11,8 @@
 coupling = 0.5
 MESH = pl.DeviceIdType.MESH
 SUBS = 2
+ONE = 5
+RING = False
 F32 = jnp.float32
 
 
@@ -31,11 +33,11 @@
     if not split or hops == 0:
         return 0
     if hops == 1:
-        return max(F * 5 // 16 // 128 * 128, 128)
+        return max(F * ONE // 16 // 128 * 128, 128)
     return F // 2 // 128 * 128
 
 
-def kernel(n, ncls, BLOCK, samples, labels_col, weight, dual, inverse,
+def kernel(n, ncls, BLOCK, samples, labels_row, weight, dual, inverse,
            new_weight, new_dual, class_gap, top_margin,
            a_all, x_buf, w_buf, gb, ib, gram, margin, sign, dual_v, alpha, change, inv_v, lab_v,
            p_buf, r_buf, gap_out, gap_in, top_out, top_in, s_out, s_all, o_buf,
@@ -47,7 +49,7 @@
     F = N // n
     width = weight.shape[1]
     par = c % 2
-    pair = c + 1 - 2 * par
+    pair = [c + 1 - 2 * par, (c - 1 + 2 * par + ncls) % ncls]
     split = ncls % 2 == 0
     peer = {d: flip(s, d, n) for d in range(1, n)}
     step_rows = rows // SUBS
@@ -96,7 +98,7 @@
 
     loads = []
     for i, (src, dst) in enumerate([(samples.at[:, cols(s * F, F)], a_all.at[s]), (weight, w_buf),
-                                    (dual, dual_v), (inverse, inv_v), (labels_col, lab_v)]):
+                                    (dual, dual_v), (inverse, inv_v), (labels_row, lab_v)]):
         load = pltpu.make_async_copy(src, dst, in_sem.at[i])
         load.start()
         loads.append(load)
@@ -121,7 +123,7 @@
         for k in range(BLOCK):
             ib[k] = jnp.broadcast_to(inv_v[:, k:k + 1], (rows, width))
         ids = c * width + lax.broadcasted_iota(jnp.int32, (rows, width), 1)
-        sign[...] = jnp.where(lab_v[...] == ids, 1.0, -1.0).astype(F32)
+        sign[...] = jnp.where(jnp.broadcast_to(lab_v[...], (width, rows)).T == ids, 1.0, -1.0).astype(F32)
         alpha[...] = dual_v[...]
         change[...] = jnp.zeros((rows, width), F32)
 
@@ -135,13 +137,29 @@
 
     partial_copy = {}
 
-    def partial_of(d):
-        if d in direct_copy:
-            direct_copy[d].wait_recv()
-        if shares(d, F, split):
+    def product(d, low, size):
+        here = cols(low, size)
+        return jnp.dot(a_all[peer[d], :, here], w_buf[here, :], preferred_element_type=F32)
+
+    def early(d):
+        h = shares(d, F, split)
+        if 2 * h == F:
+            p_buf[d] = product(d, par * h, h)
+        elif h:
             for k in range(SUBS):
                 fwd_copy[d, k].wait_recv()
-        p_buf[d] = jnp.dot(a_all[peer[d]], w_buf[...], preferred_element_type=F32)
+            p_buf[d] = product(d, 0, 2 * h)
+
+    def late(d):
+        h = shares(d, F, split)
+        if 2 * h == F:
+            for k in range(SUBS):
+                fwd_copy[d, k].wait_recv()
+            p_buf[d] = p_buf[d] + product(d, (1 - par) * h, h)
+        else:
+            direct_copy[d].wait_recv()
+            rest = product(d, 2 * h, F - 2 * h)
+            p_buf[d] = p_buf[d] + rest if h else rest
         copy = remote(p_buf.at[d], r_buf.at[d], send_p.at[d], recv_p.at[d], (peer[d], c))
         copy.start()
         partial_copy[d] = copy
@@ -153,7 +171,7 @@
         rs = pl.ds(k * step_rows, step_rows)
         split_copy[d, k].wait_recv()
         src = a_all.at[peer[d], rs, cols(par * h, h)]
-        copy = remote(src, src, send_fwd.at[d, k], recv_fwd.at[d, k], (s, pair))
+        copy = remote(src, src, send_fwd.at[d, k], recv_fwd.at[d, k], (s, pair[k % 2 if RING else 0]))
         copy.start()
         fwd_copy[d, k] = copy
         for _ in range(per):
@@ -161,23 +179,19 @@
                 work.pop(0)()
     while work:
         work.pop(0)()
-    for d in near + one_hop + far:
-        partial_of(d)
+    for d in near:
+        late(d)
+    for d in far + one_hop:
+        early(d)
+    for d in far + one_hop:
+        late(d)
 
     start = p_buf[0]
     for d in range(1, n):
         partial_copy[d].wait_recv()
         start = start + r_buf[d]
     margin[...] = start
-    scaled = sign[...] * start
-    terms = jnp.maximum(0.0, 1.0 - scaled) + dual_v[...] * (scaled - 1.0)
-    gap = jnp.sum(terms, axis=0, keepdims=True)
-    gap_out[...] = jnp.broadcast_to(gap, gap_out.shape)
-    gap_copy = []
-    for d in range(1, n):
-        copy = remote(gap_out, gap_in.at[d], send_g.at[d], recv_g.at[d], (peer[d], c))
-        copy.start()
-        gap_copy.append(copy)
+    p_buf[0] = start
 
     blocks = rows // BLOCK
 
@@ -209,6 +223,15 @@
         copy.start()
         step_copy.append(copy)
     s_all[s] = s_out[...]
+    scaled = sign[...] * p_buf[0]
+    terms = jnp.maximum(0.0, 1.0 - scaled) + dual_v[...] * (scaled - 1.0)
+    gap = jnp.sum(terms, axis=0, keepdims=True)
+    gap_out[...] = jnp.broadcast_to(gap, gap_out.shape)
+    gap_copy = []
+    for d in range(1, n):
+        copy = remote(gap_out, gap_in.at[d], send_g.at[d], recv_g.at[d], (peer[d], c))
+        copy.start()
+        gap_copy.append(copy)
     top = jnp.max(margin[...].T, axis=0, keepdims=True)
     top_out[...] = jnp.broadcast_to(top, top_out.shape)
     top_copy = []
@@ -272,7 +295,7 @@
             pltpu.VMEM((F, width), jnp.bfloat16),
             pltpu.VMEM((rows, rows, width), F32), pltpu.VMEM((block, rows, width), F32),
             pltpu.VMEM((rows, rows), F32), square, square, square, square, square,
-            pltpu.VMEM((rows, block), F32), pltpu.VMEM((rows, 1), jnp.int32),
+            pltpu.VMEM((rows, block), F32), pltpu.VMEM((1, rows), jnp.int32),
             pltpu.VMEM((n, rows, width), F32), pltpu.VMEM((n, rows, width), F32),
             pltpu.VMEM((8, width), F32), pltpu.VMEM((n, 8, width), F32),
             pltpu.VMEM((8, rows), F32), pltpu.VMEM((ncls, 8, rows), F32),
@@ -284,7 +307,7 @@
         ],
         compiler_params=pltpu.CompilerParams(collective_id=0, has_side_effects=True,
                                              vmem_limit_bytes=60 * 2 ** 20),
-    )(samples, labels[:, None], weight, dual, inverse)
+    )(samples, labels[None, :], weight, dual, inverse)
     new_weight, new_dual, gap, top = outs
     return new_weight, new_dual, gap.reshape(-1), top.reshape(-1)
 

time: 86 us -> 83.5 us (0.971)
  local copies, waits for them, and re-layouts: 6.11 us -> 4.72 us
  Pallas kernels: 79.1 us -> 78 us
    broadcast_in_dim x1 -> x0, local copies, waits for them, and re-layouts: 1.39 us -> none  [fused(): labels[:, None]]
    pallas_call x1, Pallas kernels: 79.1 us -> 78 us  [fused(): pl.pallas_call(functools.partial(kernel, n, ncls, block), out_shape=(jax....]
where the time goes in v2:
time: 83.5 us; the launch traced here: 83.4 us
  Pallas kernels  78 us (93%)
  local copies, waits for them, and re-layouts  4.72 us (6%)
    pallas_call x1, Pallas kernels, fused(): pl.pallas_call(functools.partial(kernel, n, ncls, block), out_shape=(jax....  78 us
    unnamed x10, local copies, waits for them, and re-layouts  4.72 us

profile of v2, /device:TPU:0, one launch (start us, length us, event | category | flops | bytes accessed | tf_op | source)
XLA Modules:
  0.0 83.4 jit_solution(14722091867355637395)
XLA Ops:
  0.6 78.0 %shard_map.84 = (f32[4096,128]{1,0:T(8,128)}, f32[128,128]{1,0:T(8,128)}, f32[1,128]{1,0:T(1,128)}, f32[1,128]{1,0:T(1,128)}) custom-call(bf16[128,32768]{1,0:T(8,128)(2,1)} %samples.1, s32[1,128]{1,0:T(1,128)} %bitcast.5, bf16[4096,128]{1,0:T(8,128)(2,1)} %weight.1, f32[128,128]{1,0:T(8,128)} %dual.1, f32[128,16]{1,0:T(8,128)} %bitcast.4), custom_call_target="tpu_custom_call" | custom-call | tf_op jit(solution)/shard_map/pallas_call | solution.py:287
  78.6 0.0 copy-start
  78.6 0.0 copy-start.2
  78.6 0.0 copy-start.1
  78.7 3.1 %copy.13 = f32[4096,128]{1,0:T(8,128)} copy(f32[4096,128]{1,0:T(8,128)} %get-tuple-element.16) | data formatting | bytes 4194304
  81.7 0.0 copy-done
  81.7 0.6 copy.14
  82.3 0.0 copy-done.2
  82.3 0.5 copy.15
  82.9 0.0 copy-done.1
  82.9 0.5 copy.16
Async XLA Ops:
  78.6 3.1 %copy-start = (f32[128,128]{1,0:T(8,128)S(1)}, f32[128,128]{1,0:T(8,128)}, u32[]{:S(2)}) copy-start(f32[128,128]{1,0:T(8,128)} %get-tuple-element.17) | copy-start | bytes 196612
  78.6 3.7 %copy-start.2 = (f32[1,128]{1,0:T(1,128)S(1)}, f32[1,128]{1,0:T(1,128)}, u32[]{:S(2)}) copy-start(f32[1,128]{1,0:T(1,128)} %get-tuple-element.10) | copy-start | bytes 1540
  78.6 4.2 %copy-start.1 = (f32[1,128]{1,0:T(1,128)S(1)}, f32[1,128]{1,0:T(1,128)}, u32[]{:S(2)}) copy-start(f32[1,128]{1,0:T(1,128)} %get-tuple-element.11) | copy-start | bytes 1540
